TPU v7x, 256 devices: a whole 4x4x8 slice. The times are simulated.
256 devices in a mesh: dp: 64 (over z, x, y_hi), tensor: 4 (over y_lo, core).
Axes of the slice: x: 4, y: 4 (y_hi: 2, y_lo: 2; y = y_hi * 2 + y_lo), z: 8, core: 2. Of those that a mesh axis runs over, the one named last changes fastest.
Arguments:
- d_out: bfloat16 [16384, 3072], P('dp'), may hold values from -12 to 12
- gate: bfloat16 [16384, 4096], P('dp', 'tensor'), may hold values from -16 to 16
- up_proj: bfloat16 [16384, 4096], P('dp', 'tensor'), may hold values from -12 to 12
- master: float32 [4096, 3072], P(('tensor', 'dp')), may hold values from -0.09375 to 0.09375
- moment_one: float32 [4096, 3072], P(('tensor', 'dp')), may hold values from -4 to 4
- moment_two: float32 [4096, 3072], P(('tensor', 'dp')), may hold values from 0.05 to 2
Outputs:
- gate_grad: bfloat16 [16384, 4096], P('dp', 'tensor')
- up_grad: bfloat16 [16384, 4096], P('dp', 'tensor')
- master_next: float32 [4096, 3072], P(('tensor', 'dp'))
- moment_one_next: float32 [4096, 3072], P(('tensor', 'dp'))
- moment_two_next: float32 [4096, 3072], P(('tensor', 'dp'))
- weight_next: bfloat16 [4096, 3072], P('tensor')
All inputs are finite; a program needn't handle non-finite values.
Results may differ from a plain program's by a relative error of at most 0.005.
Values may be sent and summed in bfloat16 or wider, within the bound.
A program may use at most 64 MiB of HBM per device.

v0:
```python
import jax
import jax.numpy as jnp
from jax import lax
from jax.sharding import PartitionSpec as P

D = 3072
FF = 4096


def on_device(d_out, gate, up_proj, master, moment_one, moment_two):
    weight = master.astype(jnp.bfloat16)
    gate_f = gate.astype(jnp.float32)
    up_f = up_proj.astype(jnp.float32)
    silu_gate = jax.nn.silu(gate_f)
    hidden = (silu_gate * up_f).astype(jnp.bfloat16)
    d_hidden = lax.dot_general(
        d_out,
        lax.all_gather(weight, "dp", axis=0, tiled=True),
        (((1,), (1,)), ((), ())),
        preferred_element_type=jnp.float32,
    )
    partial_term = lax.dot_general(
        hidden, d_out, (((0,), (0,)), ((), ())), preferred_element_type=jnp.float32
    )
    grad = lax.psum_scatter(partial_term, "dp", scatter_dimension=0, tiled=True)
    up_grad = (d_hidden * silu_gate).astype(jnp.bfloat16)
    sigm = jax.nn.sigmoid(gate_f)
    gate_grad = (d_hidden * up_f * sigm * (1.0 + gate_f * (1.0 - sigm))).astype(jnp.bfloat16)
    local_squares = jnp.sum(grad * grad)
    total = lax.psum(local_squares, ("dp", "tensor"))
    factor = 1.0 / jnp.sqrt(total / (FF * D) + 1e-06)
    clipped = grad * factor
    moment_one_next = 0.9 * moment_one + 0.1 * clipped
    moment_two_next = 0.95 * moment_two + 0.05 * clipped * clipped
    master_next = master - 0.003 * (
        moment_one_next / (jnp.sqrt(moment_two_next) + 1e-08) + 0.1 * master
    )
    shard_next = master_next.astype(jnp.bfloat16)
    weight_next = lax.all_gather(shard_next, "dp", axis=0, tiled=True)
    return (gate_grad, up_grad, master_next, moment_one_next, moment_two_next, weight_next)


def solution(mesh):
    placed = (
        P("dp", None),
        P("dp", "tensor"),
        P("dp", "tensor"),
        P(("tensor", "dp"), None),
        P(("tensor", "dp"), None),
        P(("tensor", "dp"), None),
    )
    return jax.shard_map(
        on_device,
        mesh=mesh,
        in_specs=placed,
        out_specs=(
            P("dp", "tensor"),
            P("dp", "tensor"),
            P(("tensor", "dp"), None),
            P(("tensor", "dp"), None),
            P(("tensor", "dp"), None),
            P("tensor", None),
        ),
        check_vma=False,
    )
```

profile of v0, /device:TPU:2, one launch (start us, length us, event | category | flops | bytes accessed | tf_op | source)
XLA Modules:
  0.0 1212.7 jit_solution(3031577703967708781)
XLA Ops:
  7.2 0.0 copy-start
  7.2 0.0 reduce-scatter.2.cloned.1.call-start
  7.2 1.4 copy-done
  8.6 7.7 fusion.8
  16.3 0.0 copy-start.3
  16.3 0.0 copy-start.4
  16.3 0.0 copy-start.5
  16.3 0.0 copy-start.1
  16.3 0.0 copy-start.2
  16.3 0.0 reduce-scatter.2.cloned.1.call-update
  16.3 0.0 all-gather.3.cloned.1.call-start
  16.4 833.1 %reduce-scatter.2.cloned.1.call-done = f32[16,3072]{1,0:T(8,128)} async-done(((f32[1024,3072]{1,0:T(8,128)}), f32[16,3072]{1,0:T(8,128)}) %reduce-scatter.2.cloned.1.call-update) | async-done | bytes 196624 | tf_op jit(solution)/shard_map/reduce_scatter | solution.py:25
  849.5 1.6 multiply_reduce_fusion
  851.1 72.7 %psum.7 = f32[]{:T(128)} all-reduce(f32[]{:T(128)} %multiply_reduce_fusion), channel_id=1, replica_groups=mesh['dp'=64,'tensor'=4] {'dp','tensor'}, use_global_device_ids=true, to_apply=%region_2.3 | all-reduce | flops 1 | bytes 8 | tf_op jit(solution)/shard_map/psum | solution.py:30
  924.4 0.0 copy-done.3
  924.4 0.0 copy-done.4
  924.4 0.0 copy-done.5
  924.5 1.9 fusion.12
  926.3 0.0 all-gather.3.cloned.1.call-update
  926.3 0.0 all-gather.5.cloned.1.call-start
  926.4 0.7 all-gather.5.cloned.1.call-update
  927.1 134.7 %all-gather.3.cloned.1.call-done = bf16[1024,3072]{1,0:T(8,128)(2,1)} async-done(((bf16[16,3072]{1,0:T(8,128)(2,1)}), bf16[1024,3072]{1,0:T(8,128)(2,1)}) %all-gather.3.cloned.1.call-update) | async-done | bytes 6291472 | tf_op jit(solution)/shard_map/all_gather | solution.py:18
  1061.7 0.0 copy-done.1
  1061.7 0.0 copy-done.2
  1061.7 5.9 multiply_convert_fusion
  1067.6 132.6 %all-gather.5.cloned.1.call-done = bf16[1024,3072]{1,0:T(8,128)(2,1)} async-done(((bf16[16,3072]{1,0:T(8,128)(2,1)}), bf16[1024,3072]{1,0:T(8,128)(2,1)}) %all-gather.5.cloned.1.call-update) | async-done | bytes 6291472 | tf_op jit(solution)/shard_map/all_gather | solution.py:39
  1200.2 5.9 copy.13
Async XLA Ops:
  7.2 1.4 copy-start
  7.2 842.3 %reduce-scatter.2.cloned.1.call-start = ((), (), s32[]{:S(2)}) async-start(), calls=%async_computation.2 | async-start | bytes 12779520 | tf_op jit(solution)/shard_map/reduce_scatter | solution.py:25
  16.3 908.2 %copy-start.3 = (f32[16,3072]{1,0:T(8,128)S(1)}, f32[16,3072]{1,0:T(8,128)}, u32[]{:S(2)}) copy-start(f32[16,3072]{1,0:T(8,128)} %param.9) | copy-start | bytes 589828
  16.3 908.2 %copy-start.4 = (f32[16,3072]{1,0:T(8,128)S(1)}, f32[16,3072]{1,0:T(8,128)}, u32[]{:S(2)}) copy-start(f32[16,3072]{1,0:T(8,128)} %param.11) | copy-start | bytes 589828
  16.3 908.2 %copy-start.5 = (f32[16,3072]{1,0:T(8,128)S(1)}, f32[16,3072]{1,0:T(8,128)}, u32[]{:S(2)}) copy-start(f32[16,3072]{1,0:T(8,128)} %param.10) | copy-start | bytes 589828
  16.3 1045.5 %copy-start.1 = (bf16[256,1024]{1,0:T(8,128)(2,1)S(1)}, bf16[256,1024]{1,0:T(8,128)(2,1)}, u32[]{:S(2)}) copy-start(bf16[256,1024]{1,0:T(8,128)(2,1)} %param.7) | copy-start | bytes 1572868
  16.3 1045.5 %copy-start.2 = (bf16[256,1024]{1,0:T(8,128)(2,1)S(1)}, bf16[256,1024]{1,0:T(8,128)(2,1)}, u32[]{:S(2)}) copy-start(bf16[256,1024]{1,0:T(8,128)(2,1)} %param.8) | copy-start | bytes 1572868
  16.3 1045.4 %all-gather.3.cloned.1.call-start = ((), (), s32[]{:S(2)}) async-start(), calls=%async_computation.1 | async-start | bytes 6389760 | tf_op jit(solution)/shard_map/all_gather | solution.py:18
  926.3 273.9 %all-gather.5.cloned.1.call-start = ((), (), s32[]{:S(2)}) async-start(), calls=%async_computation.3 | async-start | bytes 6389760 | tf_op jit(solution)/shard_map/all_gather | solution.py:39
Sparse Core Ops, SparseCore 0:
  16.4 832.9 reduce-scatter.1
  926.5 135.2 all-gather.2
  1066.6 133.6 all-gather.4
where the time goes:
time: 1210 us
  waiting for transfers between devices  1100 us (91%)
  blocking collectives  72.7 us (6%)
  between operations  14.5 us (1%)
  matrix products  13.6 us (1%)
    reduce_scatter x1, waiting for transfers between devices, on_device(): grad = lax.psum_scatter(partial_term, 'dp', scatter_dimension=0, tiled=True)  833 us
    all_gather x1, waiting for transfers between devices, on_device(): lax.all_gather(weight, 'dp', axis=0, tiled=True)  135 us
    all_gather x1, waiting for transfers between devices, on_device(): weight_next = lax.all_gather(shard_next, 'dp', axis=0, tiled=True)  133 us
    psum x1, blocking collectives, on_device(): total = lax.psum(local_squares, ('dp', 'tensor'))  72.7 us
  transfers between devices with their start and end apart: 3, of which 3 were waited for; matrix products, arithmetic and copies ran while one was open for 0% of the time, Pallas kernels for 0%

commit v1 on v0

--- a/solution.py
+++ b/solution.py
@@ -36,7 +36,9 @@
         moment_one_next / (jnp.sqrt(moment_two_next) + 1e-08) + 0.1 * master
     )
     shard_next = master_next.astype(jnp.bfloat16)
-    weight_next = lax.all_gather(shard_next, "dp", axis=0, tiled=True)
+    weight_next = jnp.concatenate(
+        lax.all_to_all(jnp.stack([shard_next] * lax.axis_size("dp")), "dp", 0, 0), axis=0
+    )
     return (gate_grad, up_grad, master_next, moment_one_next, moment_two_next, weight_next)
 
 

time: 1210 us -> 1140 us (0.942)
  waiting for transfers between devices: 1100 us -> 1010 us
    all_to_all x0 -> x1, waiting for transfers between devices: none -> 151 us  [on_device(): lax.all_to_all(jnp.stack([shard_next] * lax.axis_size('dp')), 'dp', 0, 0)]
    all_gather x1 -> x0, waiting for transfers between devices: 133 us -> none  [on_device(): weight_next = lax.all_gather(shard_next, 'dp', axis=0, tiled=True)]
    all_gather x1, waiting for transfers between devices: 135 us -> 26 us  [on_device(): lax.all_gather(weight, 'dp', axis=0, tiled=True)]
where the time goes in v1:
time: 1140 us
  waiting for transfers between devices  1010 us (89%)
  blocking collectives  72.7 us (6%)
  between operations  14.8 us (1%)
  matrix products  13.6 us (1%)
    reduce_scatter x1, waiting for transfers between devices, on_device(): grad = lax.psum_scatter(partial_term, 'dp', scatter_dimension=0, tiled=True)  833 us
    all_to_all x1, waiting for transfers between devices, on_device(): lax.all_to_all(jnp.stack([shard_next] * lax.axis_size('dp')), 'dp', 0, 0)  151 us
    psum x1, blocking collectives, on_device(): total = lax.psum(local_squares, ('dp', 'tensor'))  72.7 us
    all_gather x1, waiting for transfers between devices, on_device(): lax.all_gather(weight, 'dp', axis=0, tiled=True)  26 us
  transfers between devices with their start and end apart: 3, of which 3 were waited for; matrix products, arithmetic and copies ran while one was open for 0% of the time, Pallas kernels for 0%

profile of v1, /device:TPU:2, one launch (start us, length us, event | category | flops | bytes accessed | tf_op | source)
XLA Modules:
  0.0 1136.5 jit_solution(1216332437341925912)
XLA Ops:
  7.2 0.0 copy-start
  7.2 0.0 reduce-scatter.2.cloned.1.call-start
  7.2 1.4 copy-done
  8.6 7.7 fusion.8
  16.3 0.0 copy-start.3
  16.3 0.0 copy-start.4
  16.3 0.0 copy-start.5
  16.3 0.0 reduce-scatter.2.cloned.1.call-update
  16.3 833.2 %reduce-scatter.2.cloned.1.call-done = f32[16,3072]{1,0:T(8,128)} async-done(((f32[1024,3072]{1,0:T(8,128)}), f32[16,3072]{1,0:T(8,128)}) %reduce-scatter.2.cloned.1.call-update) | async-done | bytes 196624 | tf_op jit(solution)/shard_map/reduce_scatter | solution.py:25
  849.5 1.6 multiply_reduce_fusion
  851.0 72.7 %psum.7 = f32[]{:T(128)} all-reduce(f32[]{:T(128)} %multiply_reduce_fusion), channel_id=1, replica_groups=mesh['dp'=64,'tensor'=4] {'dp','tensor'}, use_global_device_ids=true, to_apply=%region_2.3 | all-reduce | flops 1 | bytes 8 | tf_op jit(solution)/shard_map/psum | solution.py:30
  924.4 0.0 copy-done.3
  924.4 0.0 copy-done.4
  924.4 0.0 copy-done.5
  924.4 1.8 fusion.12
  926.3 3.5 stack.2
  929.8 0.0 copy-start.1
  929.8 0.0 copy-start.2
  929.8 10.0 all-to-all-start
  939.8 0.0 all-gather.2.cloned.1.call-start
  939.8 0.7 all-gather.2.cloned.1.call-update
  940.5 151.3 %all-to-all-done = bf16[64,16,3072]{2,1,0:T(8,128)(2,1)} async-done(((bf16[64,16,3072]{2,1,0:T(8,128)(2,1)}), bf16[64,16,3072]{2,1,0:T(8,128)(2,1)}, u32[]{:S(2)}, u32[]{:S(2)}) %all-to-all-start) | async-done | bytes 6291488 | tf_op jit(solution)/shard_map/all_to_all | solution.py:40
  1091.8 26.0 %all-gather.2.cloned.1.call-done = bf16[1024,3072]{1,0:T(8,128)(2,1)} async-done(((bf16[16,3072]{1,0:T(8,128)(2,1)}), bf16[1024,3072]{1,0:T(8,128)(2,1)}) %all-gather.2.cloned.1.call-update) | async-done | bytes 6291472 | tf_op jit(solution)/shard_map/all_gather | solution.py:18
  1117.8 0.0 copy-done.1
  1117.8 0.0 copy-done.2
  1117.8 5.9 multiply_convert_fusion
  1123.7 5.9 copy.13
Async XLA Ops:
  7.2 1.4 copy-start
  7.2 842.3 %reduce-scatter.2.cloned.1.call-start = ((), (), s32[]{:S(2)}) async-start(), calls=%async_computation.3 | async-start | bytes 12779520 | tf_op jit(solution)/shard_map/reduce_scatter | solution.py:25
  16.3 908.1 %copy-start.3 = (f32[16,3072]{1,0:T(8,128)S(1)}, f32[16,3072]{1,0:T(8,128)}, u32[]{:S(2)}) copy-start(f32[16,3072]{1,0:T(8,128)} %param.9) | copy-start | bytes 589828
  16.3 908.1 %copy-start.4 = (f32[16,3072]{1,0:T(8,128)S(1)}, f32[16,3072]{1,0:T(8,128)}, u32[]{:S(2)}) copy-start(f32[16,3072]{1,0:T(8,128)} %param.11) | copy-start | bytes 589828
  16.3 908.2 %copy-start.5 = (f32[16,3072]{1,0:T(8,128)S(1)}, f32[16,3072]{1,0:T(8,128)}, u32[]{:S(2)}) copy-start(f32[16,3072]{1,0:T(8,128)} %param.10) | copy-start | bytes 589828
  929.8 188.1 %copy-start.1 = (bf16[256,1024]{1,0:T(8,128)(2,1)S(1)}, bf16[256,1024]{1,0:T(8,128)(2,1)}, u32[]{:S(2)}) copy-start(bf16[256,1024]{1,0:T(8,128)(2,1)} %param.7) | copy-start | bytes 1572868
  929.8 188.1 %copy-start.2 = (bf16[256,1024]{1,0:T(8,128)(2,1)S(1)}, bf16[256,1024]{1,0:T(8,128)(2,1)}, u32[]{:S(2)}) copy-start(bf16[256,1024]{1,0:T(8,128)(2,1)} %param.8) | copy-start | bytes 1572868
  929.8 162.0 %all-to-all-start = ((bf16[64,16,3072]{2,1,0:T(8,128)(2,1)}), bf16[64,16,3072]{2,1,0:T(8,128)(2,1)}, u32[]{:S(2)}, u32[]{:S(2)}) async-start(bf16[64,16,3072]{2,1,0:T(8,128)(2,1)} %stack.2), calls=%async_computation.1 | async-start | bytes 12582912 | tf_op jit(solution)/shard_map/all_to_all | solution.py:40
  939.8 178.0 %all-gather.2.cloned.1.call-start = ((), (), s32[]{:S(2)}) async-start(), calls=%async_computation.2 | async-start | bytes 6389760 | tf_op jit(solution)/shard_map/all_gather | solution.py:18
Sparse Core Ops, SparseCore 0:
  16.4 832.9 reduce-scatter.1
  945.5 172.3 all-gather.1
